TPU v7x, 32 devices: a whole 2x2x4 slice. The times are simulated.
32 devices in a mesh: tp: 4 (over x, core), ep: 2 (over y), dp: 4 (over z).
Axes of the slice: x: 2, y: 2, z: 4, core: 2. Of those that a mesh axis runs over, the one named last changes fastest.
Arguments:
- tokens: bfloat16 [8, 512, 768], P(('ep', 'dp'), 'tp'), may hold values from -6 to 6
- segment: int32 [8, 512], P(('ep', 'dp')), may hold values from 0 to 7, never falling along the last dimension, each value on 1 to 256 neighbouring positions
- key_mask: int32 [8, 512], P(('ep', 'dp')), may hold values 0 or 1
- routes: int32 [8, 512, 2], P(('ep', 'dp'), 'tp'), may hold values from 0 to 3, all different within a row; in each aligned block of 128 rows (0 to 127, 128 to 255, ..., all dimensions but the last counted through in order) at most 128 rows name the same one
- gates: float32 [8, 512, 2], P(('ep', 'dp'), 'tp'), may hold values from 0.25 to 1
- ln1_gain: float32 [768], replicated, may hold values from 0.5 to 1.5
- ln1_bias: float32 [768], replicated, may hold values from -0.5 to 0.5
- query_weight: bfloat16 [768, 768], P(None, 'tp'), may hold values from -0.21875 to 0.21875
- key_weight: bfloat16 [768, 768], P(None, 'tp'), may hold values from -0.21875 to 0.21875
- value_weight: bfloat16 [768, 768], P(None, 'tp'), may hold values from -0.21875 to 0.21875
- out_weight: bfloat16 [768, 768], P('tp'), may hold values from -2.5 to 2.5
- ln2_gain: float32 [768], replicated, may hold values from 0.5 to 1.5
- ln2_bias: float32 [768], replicated, may hold values from -0.5 to 0.5
- frozen_in: bfloat16 [2, 768, 3072], P('ep'), may hold values from -0.21875 to 0.21875
- frozen_out: bfloat16 [2, 3072, 768], P('ep'), may hold values from -0.109375 to 0.109375
- train_in: bfloat16 [2, 768, 3072], P('ep'), may hold values from -0.21875 to 0.21875
- train_out: bfloat16 [2, 3072, 768], P('ep'), may hold values from -0.109375 to 0.109375
- cotangent: bfloat16 [8, 512, 768], P(('ep', 'dp'), 'tp'), may hold values from -6 to 6
Outputs:
- layer_out: bfloat16 [8, 512, 768], P(('ep', 'dp'), 'tp')
- tokens_grad: float32 [8, 512, 768], P(('ep', 'dp'), 'tp')
- ln1_gain_grad: float32 [768], replicated
- ln1_bias_grad: float32 [768], replicated
- query_grad: float32 [768, 768], P(None, 'tp')
- key_grad: float32 [768, 768], P(None, 'tp')
- value_grad: float32 [768, 768], P(None, 'tp')
- out_grad: float32 [768, 768], P('tp')
- ln2_gain_grad: float32 [768], replicated
- ln2_bias_grad: float32 [768], replicated
- train_in_grad: float32 [2, 768, 3072], P('ep')
- train_out_grad: float32 [2, 3072, 768], P('ep')
- expert_counts: int32 [4], replicated
Inputs may be any that keep to these rules, and one draw needn't show every extreme that they name: `segment`: segment numbers never fall along a group; each sequence holds 1 to 256 tokens, one exactly 256. `routes`: the two experts of a token differ. In the tokens of one device (aligned blocks of 128 tokens) no expert is named more than 128 times, a bound that some block reaches.
All inputs are finite; a program needn't handle non-finite values. No bound on the sum of `key_mask` on one device may be relied on, other than what follows from the above.
Results may differ from a plain program's by a relative error of at most 0.017.
Values may be sent and summed in bfloat16 or wider, within the bound.
A program may use at most 192 MiB of HBM per device.

v0:
```python
import jax
import jax.numpy as jnp
from jax import lax
from jax.sharding import PartitionSpec as P

HD = 64
EXP_DEV = 2
EPSILON = 1e-05
MASKED = -1e30


def layer_norm(values, gain, bias):
    center = jnp.mean(values, axis=-1, keepdims=True)
    shifted = values - center
    spread = jnp.mean(shifted * shifted, axis=-1, keepdims=True)
    return shifted * lax.rsqrt(spread + EPSILON) * gain + bias


def gelu_exact(values):
    return jax.nn.gelu(values, approximate=False)


def contract(left, right, left_dim, right_dim):
    return lax.dot_general(
        left, right, (((left_dim,), (right_dim,)), ((), ())), preferred_element_type=jnp.float32
    )


def masked_scores(queries, query_segment, keys, segment_row, keep_row):
    scale = queries.shape[-1] ** (-0.5)
    scores = jnp.einsum("hqd,hkd->hqk", queries, keys, preferred_element_type=jnp.float32) * scale
    allowed = (query_segment[:, None] == segment_row[None, :]) & keep_row[None, :]
    return jnp.where(allowed[None], scores, MASKED)


def to_owners(buffer):
    return lax.all_to_all(buffer, "ep", split_axis=0, concat_axis=0, tiled=True)


def to_sources(buffer):
    return lax.all_to_all(buffer, "ep", split_axis=0, concat_axis=0, tiled=True)


def expert_forward(inputs, inner, outer):
    hidden = contract(inputs, inner, 1, 0)
    active = gelu_exact(hidden).astype(jnp.bfloat16)
    return (hidden, active, contract(active, outer, 1, 0))


def expert_backward(inputs, hidden, active, upstream, inner, outer, trainable):
    through = contract(upstream, outer, 1, 1)
    slope = jax.vjp(gelu_exact, hidden)[1](through)[0].astype(jnp.bfloat16)
    back_in = contract(slope, inner, 1, 1)
    if trainable:
        return (back_in, contract(inputs, slope, 0, 0), contract(active, upstream, 0, 0))
    return (back_in, None, None)


def local(
    tokens,
    segment,
    key_mask,
    routes,
    gates,
    ln1_gain,
    ln1_bias,
    query_weight,
    key_weight,
    value_weight,
    out_weight,
    ln2_gain,
    ln2_bias,
    frozen_in,
    frozen_out,
    train_in,
    train_out,
    cotangent,
):
    tp_count = lax.axis_size("tp")
    ep_count = lax.axis_size("ep")
    local_rows = tokens.shape[1]
    width = tokens.shape[2]
    group_rows = local_rows * tp_count
    head_cols = query_weight.shape[1]
    local_heads = head_cols // HD
    residual = tokens[0].astype(jnp.float32)
    joined = jnp.concatenate([query_weight, key_weight, value_weight], axis=1)
    first_normed = layer_norm(residual, ln1_gain, ln1_bias).astype(jnp.bfloat16)
    piece = lax.all_gather(first_normed, "tp", axis=0, tiled=True)
    projected = contract(piece, joined, 1, 0)
    gathered = piece
    projected, normed_group = (projected, gathered)
    projected = projected.astype(jnp.bfloat16)
    block = min(512, group_rows)
    blocks = group_rows // block

    def split_heads(matrix):
        return matrix.reshape(group_rows, local_heads, HD).transpose(1, 0, 2)

    def merge_heads(tensor):
        return tensor.transpose(1, 0, 2).reshape(group_rows, head_cols)

    queries = split_heads(projected[:, :head_cols])
    keys = split_heads(projected[:, head_cols : 2 * head_cols])
    values = split_heads(projected[:, 2 * head_cols :])
    query_blocks = queries.reshape(local_heads, blocks, block, HD).transpose(1, 0, 2, 3)
    segment_row = segment[0]
    starts = jnp.concatenate(
        [segment_row[:1] == segment_row[:1], segment_row[1:] != segment_row[:-1]]
    )
    keep_row = (key_mask[0] == 1) | starts
    segment_blocks = segment_row.reshape(blocks, block)

    def forward_block(item):
        block_queries, block_segment = item
        scores = masked_scores(block_queries, block_segment, keys, segment_row, keep_row)
        highest = jnp.max(scores, axis=-1, keepdims=True)
        weights = jnp.exp(scores - highest)
        totals = jnp.sum(weights, axis=-1, keepdims=True)
        probs = (weights / totals).astype(jnp.bfloat16)
        outputs = jnp.einsum("hqk,hkd->hqd", probs, values, preferred_element_type=jnp.float32)
        return (outputs, (highest + jnp.log(totals))[..., 0])

    head_blocks, log_totals = lax.map(forward_block, (query_blocks, segment_blocks))
    attn_heads = (
        head_blocks.transpose(0, 2, 1, 3).reshape(group_rows, head_cols).astype(jnp.bfloat16)
    )
    middle = residual + lax.psum_scatter(
        contract(attn_heads, out_weight, 1, 0), "tp", scatter_dimension=0, tiled=True
    )
    second_normed = layer_norm(middle, ln2_gain, ln2_bias).astype(jnp.bfloat16)
    experts = EXP_DEV * ep_count
    capacity = 4 * local_rows // experts
    slots = experts * capacity
    route = routes[0]
    marks = (route.reshape(-1)[:, None] == jnp.arange(experts, dtype=jnp.int32)[None, :]).astype(
        jnp.int32
    )
    places = jnp.sum((jnp.cumsum(marks, axis=0) - 1) * marks, axis=1).reshape(local_rows, 2)
    slot_ids = route * capacity + places
    slot_range = jnp.arange(slots, dtype=jnp.int32)[None, :]
    pick_first = (slot_ids[:, 0:1] == slot_range).astype(jnp.bfloat16)
    pick_second = (slot_ids[:, 1:2] == slot_range).astype(jnp.bfloat16)
    local_counts = jnp.sum(marks, axis=0).astype(jnp.float32)
    send = contract(pick_first + pick_second, second_normed, 0, 0).astype(jnp.bfloat16)
    arrived = to_owners(send.reshape(ep_count, EXP_DEV, capacity, width))
    inner_list = (frozen_in[0], train_in[0])
    outer_list = (frozen_out[0], train_out[0])
    kept = []
    produced = []
    for index in range(EXP_DEV):
        inputs = arrived[:, index].reshape(-1, width)
        hidden, active, result = expert_forward(inputs, inner_list[index], outer_list[index])
        kept.append((inputs, hidden, active))
        produced.append(result.reshape(ep_count, -1, width))
    produced = jnp.stack(produced, axis=1)
    returned = to_sources(produced.astype(jnp.bfloat16)).reshape(slots, width)
    gate_rows = gates[0]
    mixture = gate_rows[:, 0:1] * contract(pick_first, returned, 1, 0) + gate_rows[
        :, 1:2
    ] * contract(pick_second, returned, 1, 0)
    layer_out = (middle + mixture).astype(jnp.bfloat16)
    upstream = cotangent[0].astype(jnp.float32)
    first_share = (gate_rows[:, 0:1] * upstream).astype(jnp.bfloat16)
    second_share = (gate_rows[:, 1:2] * upstream).astype(jnp.bfloat16)
    back_send = (
        contract(pick_first, first_share, 0, 0) + contract(pick_second, second_share, 0, 0)
    ).astype(jnp.bfloat16)
    back_arrived = to_owners(back_send.reshape(ep_count, EXP_DEV, capacity, width))
    input_terms = []
    grad_in = None
    grad_out = None
    for index in range(EXP_DEV):
        inputs, hidden, active = kept[index]
        back_in, maybe_in, maybe_out = expert_backward(
            inputs,
            hidden,
            active,
            back_arrived[:, index].reshape(-1, width),
            inner_list[index],
            outer_list[index],
            index == EXP_DEV - 1,
        )
        if index == EXP_DEV - 1:
            grad_in, grad_out = (maybe_in, maybe_out)
        input_terms.append(back_in.reshape(ep_count, -1, width))
    input_terms = jnp.stack(input_terms, axis=1)
    back_returned = to_sources(input_terms.astype(jnp.bfloat16)).reshape(slots, width)
    grad_in, grad_out = (
        lax.psum(grad_in.astype(jnp.bfloat16), ("tp", "dp")).astype(jnp.float32),
        lax.psum(grad_out.astype(jnp.bfloat16), ("tp", "dp")).astype(jnp.float32),
    )
    second_grad = contract(pick_first, back_returned, 1, 0) + contract(
        pick_second, back_returned, 1, 0
    )
    middle_part, ln2_gain_grad, ln2_bias_grad = jax.vjp(layer_norm, middle, ln2_gain, ln2_bias)[1](
        second_grad
    )
    middle_grad = upstream + middle_part
    attn_grad = middle_grad.astype(jnp.bfloat16)
    piece = lax.all_gather(attn_grad, "tp", axis=0, tiled=True)
    head_grad = contract(piece, out_weight, 1, 1)
    out_part = contract(attn_heads, piece, 0, 0)
    head_grad, out_part = (head_grad, out_part)
    upstream_blocks = (
        split_heads(head_grad.astype(jnp.bfloat16))
        .reshape(local_heads, blocks, block, HD)
        .transpose(1, 0, 2, 3)
    )

    def backward_block(carry, item):
        key_sum, value_sum = carry
        block_queries, block_segment, block_totals, block_upstream = item
        scores = masked_scores(block_queries, block_segment, keys, segment_row, keep_row)
        probs = jnp.exp(scores - block_totals[..., None])
        prob_grad = jnp.einsum(
            "hqd,hkd->hqk", block_upstream, values, preferred_element_type=jnp.float32
        )
        centered = jnp.sum(probs * prob_grad, axis=-1, keepdims=True)
        score_grad = (probs * (prob_grad - centered)).astype(jnp.bfloat16)
        scale = block_queries.shape[-1] ** (-0.5)
        query_part = (
            jnp.einsum("hqk,hkd->hqd", score_grad, keys, preferred_element_type=jnp.float32) * scale
        )
        key_sum = (
            key_sum
            + jnp.einsum(
                "hqk,hqd->hkd", score_grad, block_queries, preferred_element_type=jnp.float32
            )
            * scale
        )
        value_sum = value_sum + jnp.einsum(
            "hqk,hqd->hkd",
            probs.astype(jnp.bfloat16),
            block_upstream,
            preferred_element_type=jnp.float32,
        )
        return ((key_sum, value_sum), query_part)

    zero_heads = jnp.zeros((local_heads, group_rows, HD), jnp.float32)
    (key_sum, value_sum), query_parts = lax.scan(
        backward_block,
        (zero_heads, zero_heads),
        (query_blocks, segment_blocks, log_totals, upstream_blocks),
    )
    query_full = query_parts.transpose(0, 2, 1, 3).reshape(group_rows, head_cols)
    projected_grad = jnp.concatenate(
        [query_full, merge_heads(key_sum), merge_heads(value_sum)], axis=1
    ).astype(jnp.bfloat16)
    joined_grad = contract(normed_group, projected_grad, 0, 0)
    first_grad = lax.psum_scatter(
        contract(projected_grad, joined, 1, 1).astype(jnp.bfloat16),
        "tp",
        scatter_dimension=0,
        tiled=True,
    ).astype(jnp.float32)
    residual_part, ln1_gain_grad, ln1_bias_grad = jax.vjp(layer_norm, residual, ln1_gain, ln1_bias)[
        1
    ](first_grad)
    tokens_grad = middle_grad + residual_part
    summed = (
        lax.psum(joined_grad[:, :head_cols].astype(jnp.bfloat16), ("ep", "dp")).astype(jnp.float32),
        lax.psum(
            joined_grad[:, head_cols : 2 * head_cols].astype(jnp.bfloat16), ("ep", "dp")
        ).astype(jnp.float32),
        lax.psum(joined_grad[:, 2 * head_cols :].astype(jnp.bfloat16), ("ep", "dp")).astype(
            jnp.float32
        ),
        lax.psum(out_part.astype(jnp.bfloat16), ("ep", "dp")).astype(jnp.float32),
    )
    counts, gain_one, bias_one, gain_two, bias_two = lax.psum(
        (local_counts, ln1_gain_grad, ln1_bias_grad, ln2_gain_grad, ln2_bias_grad),
        ("tp", "ep", "dp"),
    )
    return (
        layer_out[None],
        tokens_grad[None],
        gain_one,
        bias_one,
        summed[0],
        summed[1],
        summed[2],
        summed[3],
        gain_two,
        bias_two,
        grad_in[None],
        grad_out[None],
        counts.astype(jnp.int32),
    )


def solution(mesh):
    in_specs = (
        P(("ep", "dp"), "tp", None),
        P(("ep", "dp"), None),
        P(("ep", "dp"), None),
        P(("ep", "dp"), "tp", None),
        P(("ep", "dp"), "tp", None),
        P(),
        P(),
        P(None, "tp"),
        P(None, "tp"),
        P(None, "tp"),
        P("tp", None),
        P(),
        P(),
        P("ep", None, None),
        P("ep", None, None),
        P("ep", None, None),
        P("ep", None, None),
        P(("ep", "dp"), "tp", None),
    )
    out_specs = (
        P(("ep", "dp"), "tp", None),
        P(("ep", "dp"), "tp", None),
        P(),
        P(),
        P(None, "tp"),
        P(None, "tp"),
        P(None, "tp"),
        P("tp", None),
        P(),
        P(),
        P("ep", None, None),
        P("ep", None, None),
        P(),
    )
    return jax.shard_map(local, mesh=mesh, in_specs=in_specs, out_specs=out_specs, check_vma=False)
```

profile of v0, /device:TPU:0, one launch (start us, length us, event | category | flops | bytes accessed | tf_op | source)
XLA Modules:
  0.0 457.1 jit_solution(4886164368282397368)
XLA Ops:
  12.2 10.1 %all_gather.6 = bf16[512,768]{1,0:T(8,128)(2,1)S(1)} all-gather(bf16[128,768]{1,0:T(8,128)(2,1)S(1)} %fusion.83), channel_id=1, replica_groups=mesh['tp'=4,'ep'=2,'dp'=4] {'tp'}, dimensions={0}, use_global_device_ids=true | all-gather | bytes 983040 | tf_op jit(solution)/shard_map/all_gather | solution.py:89
  36.4 2.4 add_convert_fusion.2
  38.7 4.3 all-to-all-start.2
  43.0 16.9 %reduce-scatter.3.cloned.1.call-done = f32[128,768]{1,0:T(8,128)} async-done(((f32[512,768]{1,0:T(8,128)}), f32[128,768]{1,0:T(8,128)}) %reduce-scatter.3.cloned.1.call-update) | async-done | bytes 393232 | tf_op jit(solution)/shard_map/reduce_scatter | solution.py:128
  63.2 4.5 all-to-all-start
  67.7 2.0 fusion.128
  69.8 8.8 %all-to-all-done = bf16[2,2,128,768]{3,2,1,0:T(8,128)(2,1)} async-done(((bf16[2,2,128,768]{3,2,1,0:T(8,128)(2,1)}), bf16[2,2,128,768]{3,2,1,0:T(8,128)(2,1)}, u32[]{:S(2)}, u32[]{:S(2)}) %all-to-all-start) | async-done | bytes 786464 | tf_op jit(solution)/shard_map/all_to_all | solution.py:37
  80.0 11.0 %multiply_convert_fusion.2 = (bf16[256,3072]{1,0:T(8,128)(2,1)}, f32[256,3072]{1,0:T(8,128)S(1)}, f32[256,3072]{1,0:T(8,128)S(1)}) fusion(bf16[256,768]{1,0:T(8,128)(2,1)S(1)} %bitcast.231, bf16[1,768,3072]{2,1,0:T(8,128)(2,1)} %param.31), kind=kOutput, calls=%fused_computation.42 | convolution fusion | flops 1259077632 | bytes 12976128 | tf_op jit(solution)/shard_map/dot_general | solution.py:24
  91.0 2.0 add_convert_fusion.1
  94.6 9.0 %multiply_convert_fusion.1 = (bf16[256,3072]{1,0:T(8,128)(2,1)}, f32[256,3072]{1,0:T(8,128)S(1)}, f32[256,3072]{1,0:T(8,128)S(1)}) fusion(bf16[256,768]{1,0:T(8,128)(2,1)S(1)} %bitcast.215, bf16[1,768,3072]{2,1,0:T(8,128)(2,1)S(1)} %bitcast.244), kind=kOutput, calls=%fused_computation.29 | convolution fusion | flops 1259077632 | bytes 12976128 | tf_op jit(solution)/shard_map/dot_general | solution.py:24
  103.6 2.0 add_convert_fusion
  108.1 4.3 all-to-all-start.3
  112.5 10.1 %all-to-all-done.3 = bf16[2,2,128,768]{3,2,1,0:T(8,128)(2,1)} async-done(((bf16[2,2,128,768]{3,2,1,0:T(8,128)(2,1)}), bf16[2,2,128,768]{3,2,1,0:T(8,128)(2,1)}, u32[]{:S(2)}, u32[]{:S(2)}) %all-to-all-start.3) | async-done | bytes 786464 | tf_op jit(solution)/shard_map/all_to_all | solution.py:41
  126.9 7.8 %all_gather.7 = bf16[512,768]{1,0:T(8,128)(2,1)S(1)} all-gather(bf16[128,768]{1,0:T(8,128)(2,1)S(1)} %fusion.94), channel_id=1, replica_groups=mesh['tp'=4,'ep'=2,'dp'=4] {'tp'}, dimensions={0}, use_global_device_ids=true | all-gather | bytes 983040 | tf_op jit(solution)/shard_map/all_gather | solution.py:201
  141.2 2.7 convolution_convert_fusion.3
  144.2 5.2 %fusion.16 = bf16[1,768,3072]{2,1,0:T(8,128)(2,1)} fusion(bf16[256,768]{1,0:T(8,128)(2,1)S(1)} %bitcast.216, bf16[256,3072]{1,0:T(8,128)(2,1)} %copy-done.19), kind=kOutput, calls=%fused_computation.20 | convolution fusion | flops 1210318848 | bytes 6684672 | tf_op jit(solution)/shard_map/dot_general | solution.py:24
  149.4 3.6 fusion.17
  154.5 3.7 fusion.61
  158.2 3.8 fusion.58
  163.0 3.5 all-to-all-start.1
  166.6 13.7 %all-to-all-done.1 = bf16[2,2,128,768]{3,2,1,0:T(8,128)(2,1)S(1)} async-done(((bf16[2,2,128,768]{3,2,1,0:T(8,128)(2,1)}), bf16[2,2,128,768]{3,2,1,0:T(8,128)(2,1)S(1)}, u32[]{:S(2)}, u32[]{:S(2)}) %all-to-all-start.1) | async-done | bytes 786464 | tf_op jit(solution)/shard_map/all_to_all | solution.py:41
  181.6 42.1 %all-reduce.9.cloned.1.call-done = (bf16[768,192]{0,1:T(8,128)(2,1)}, bf16[768,192]{0,1:T(8,128)(2,1)}, bf16[768,192]{0,1:T(8,128)(2,1)}, bf16[192,768]{1,0:T(8,128)(2,1)}) async-done(((bf16[768,192]{0,1:T(8,128)(2,1)}, bf16[768,192]{0,1:T(8,128)(2,1)}, bf16[768,192]{0,1:T(8,128)(2,1)}, bf16[192,768]{1,0:T(8,128)(2,1)}), (bf16[768,192]{0,1:T(8,128)(2,1)}, bf16[768,192]{0,1:T(8,128)(2,1)}, ...) | async-done | bytes 1179664 | tf_op jit(solution)/shard_map/psum | solution.py:262
  223.7 1.8 convert_element_type.162
  225.5 1.8 convert_element_type.163
  227.3 1.8 convert_element_type.164
  229.1 1.8 convert_element_type.166
  230.9 17.7 %reduce-scatter.5.cloned.1.call-done = bf16[128,768]{1,0:T(8,128)(2,1)} async-done(((bf16[512,768]{1,0:T(8,128)(2,1)}), bf16[128,768]{1,0:T(8,128)(2,1)}) %reduce-scatter.5.cloned.1.call-update) | async-done | bytes 196624 | tf_op jit(solution)/shard_map/reduce_scatter | solution.py:251
  251.0 41.6 %all-reduce.1 = (f32[768]{0:T(1024)}, f32[768]{0:T(1024)}, f32[768]{0:T(1024)}, f32[768]{0:T(1024)}, f32[4]{0:T(128)S(1)}) all-reduce(f32[768]{0:T(1024)S(1)} %get-tuple-element.61, f32[768]{0:T(1024)S(1)} %get-tuple-element.64, f32[768]{0:T(1024)S(1)} %get-tuple-element.59, ...), channel_id=1, replica_groups=mesh['tp'=4,'ep'=2,'dp'=4] {'tp','ep','dp'}, use_global_device_ids=true, to_apply=%region_17.18 | all-reduce | flops 3076 | bytes 24608 | tf_op jit(solution)/shard_map/psum | solution.py:271
  293.2 1.9 add_bitcast_fusion
  295.1 143.5 %all-reduce.7.cloned.1.call-done = (bf16[1,768,3072]{2,1,0:T(8,128)(2,1)}, bf16[1,3072,768]{2,1,0:T(8,128)(2,1)}) async-done(((bf16[1,768,3072]{2,1,0:T(8,128)(2,1)}, bf16[1,3072,768]{2,1,0:T(8,128)(2,1)}), (bf16[1,768,3072]{2,1,0:T(8,128)(2,1)}, bf16[1,3072,768]{2,1,0:T(8,128)(2,1)})) %all-reduce.7.cloned.1.call-update) | async-done | bytes 9437200 | tf_op jit(solution)/shard_map/psum | solution.py:190
  438.5 7.5 %broadcast_in_dim.113 = f32[1,768,3072]{2,1,0:T(8,128)} convert(bf16[1,768,3072]{2,1,0:T(8,128)(2,1)} %get-tuple-element.86) | non-fusion elementwise | flops 2359296 | bytes 14155776 | tf_op jit(solution)/shard_map/broadcast_in_dim | solution.py:286
  446.1 4.5 broadcast_in_dim.115
  (176 shorter events, 45.1 us)
Async XLA Ops:
  7.2 22.2 %copy-start = (bf16[192,768]{1,0:T(8,128)(2,1)S(1)}, bf16[192,768]{1,0:T(8,128)(2,1)}, u32[]{:S(2)}) copy-start(bf16[192,768]{1,0:T(8,128)(2,1)} %param.28) | copy-start | bytes 884740
  7.2 17.2 %copy-start.27 = (bf16[768,192]{0,1:T(8,128)(2,1)S(1)}, bf16[768,192]{0,1:T(8,128)(2,1)}, u32[]{:S(2)}) copy-start(bf16[768,192]{0,1:T(8,128)(2,1)} %param.27) | copy-start | bytes 884740
  7.2 52.7 %reduce-scatter.3.cloned.1.call-start = ((), (), s32[]{:S(2)}) async-start(), calls=%async_computation.6 | async-start | bytes 1966080 | tf_op jit(solution)/shard_map/reduce_scatter | solution.py:128
  12.2 14.0 %copy-start.33 = (s32[1,512]{1,0:T(1,128)S(1)}, s32[1,512]{1,0:T(1,128)}, u32[]{:S(2)}) copy-start(s32[1,512]{1,0:T(1,128)} %param.19) | copy-start | bytes 6148
  28.7 6.2 %copy-start.36 = (f32[1,128,2]{1,2,0:T(2,128)S(1)}, f32[1,128,2]{1,2,0:T(2,128)}, u32[]{:S(2)}) copy-start(f32[1,128,2]{1,2,0:T(2,128)} %param.22) | copy-start | bytes 3076
  36.3 25.5 %copy-start.32 = (f32[768]{0:T(1024)S(1)}, f32[768]{0:T(1024)}, u32[]{:S(2)}) copy-start(f32[768]{0:T(1024)} %param.29) | copy-start | bytes 9220
  36.3 25.5 %copy-start.34 = (f32[768]{0:T(1024)S(1)}, f32[768]{0:T(1024)}, u32[]{:S(2)}) copy-start(f32[768]{0:T(1024)} %param.30) | copy-start | bytes 9220
  38.7 24.5 %all-to-all-start.2 = ((bf16[2,2,128,768]{3,2,1,0:T(8,128)(2,1)}), bf16[2,2,128,768]{3,2,1,0:T(8,128)(2,1)}, u32[]{:S(2)}, u32[]{:S(2)}) async-start(bf16[2,2,128,768]{3,2,1,0:T(8,128)(2,1)} %bitcast.214), calls=%async_computation.3 | async-start | bytes 1572864 | tf_op jit(solution)/shard_map/all_to_all | solution.py:37
  63.2 15.3 %all-to-all-start = ((bf16[2,2,128,768]{3,2,1,0:T(8,128)(2,1)}), bf16[2,2,128,768]{3,2,1,0:T(8,128)(2,1)}, u32[]{:S(2)}, u32[]{:S(2)}) async-start(bf16[2,2,128,768]{3,2,1,0:T(8,128)(2,1)} %bitcast.213), calls=%async_computation.1 | async-start | bytes 1572864 | tf_op jit(solution)/shard_map/all_to_all | solution.py:37
  78.6 12.4 %slice-start.4 = ((s8[4718592]{0:T(1024)(128)(4,1)}), s8[4194304]{0:T(1024)(128)(4,1)S(1)}, s32[]{:S(2)}) async-start(s8[4718592]{0:T(1024)(128)(4,1)} %bitcast.245), calls=%async_computation.14 | async-start | bytes 8388608
  78.6 14.5 %slice-start = ((s8[4718592]{0:T(1024)(128)(4,1)}), s8[4194304]{0:T(1024)(128)(4,1)S(1)}, s32[]{:S(2)}) async-start(s8[4718592]{0:T(1024)(128)(4,1)} %bitcast.241), calls=%async_computation.10 | async-start | bytes 8388608
  78.6 15.9 %slice-start.2 = ((s8[4718592]{0:T(1024)(128)(4,1)}), s8[4194304]{0:T(1024)(128)(4,1)S(1)}, s32[]{:S(2)}) async-start(s8[4718592]{0:T(1024)(128)(4,1)} %bitcast.243), calls=%async_computation.12 | async-start | bytes 8388608
  79.9 14.6 %copy-start.11 = (bf16[2,1,128,768]{3,2,1,0:T(8,128)(2,1)}, bf16[2,1,128,768]{3,2,1,0:T(8,128)(2,1)S(1)}, u32[]{:S(2)}) copy-start(bf16[2,1,128,768]{3,2,1,0:T(8,128)(2,1)S(1)} %get-tuple-element.106) | copy-start | bytes 1179652
  79.9 11.1 %copy-start.26 = (bf16[2,1,128,768]{3,2,1,0:T(8,128)(2,1)S(1)}, bf16[2,1,128,768]{3,2,1,0:T(8,128)(2,1)}, u32[]{:S(2)}) copy-start(bf16[2,1,128,768]{3,2,1,0:T(8,128)(2,1)} %get-tuple-element.103) | copy-start | bytes 1179652
  79.9 11.1 %slice-start.5 = ((s8[4718592]{0:T(1024)(128)(4,1)}), s8[524288]{0:T(1024)(128)(4,1)S(1)}, s32[]{:S(2)}) async-start(s8[4718592]{0:T(1024)(128)(4,1)} %bitcast.245), calls=%async_computation.15 | async-start | bytes 1048576
  79.9 13.1 %slice-start.1 = ((s8[4718592]{0:T(1024)(128)(4,1)}), s8[524288]{0:T(1024)(128)(4,1)S(1)}, s32[]{:S(2)}) async-start(s8[4718592]{0:T(1024)(128)(4,1)} %bitcast.241), calls=%async_computation.11 | async-start | bytes 1048576
  79.9 14.6 %slice-start.3 = ((s8[4718592]{0:T(1024)(128)(4,1)}), s8[524288]{0:T(1024)(128)(4,1)S(1)}, s32[]{:S(2)}) async-start(s8[4718592]{0:T(1024)(128)(4,1)} %bitcast.243), calls=%async_computation.13 | async-start | bytes 1048576
  93.0 10.5 %slice-start.6 = ((s8[4718592]{0:T(1024)(128)(4,1)}), s8[4194304]{0:T(1024)(128)(4,1)S(1)}, s32[]{:S(2)}) async-start(s8[4718592]{0:T(1024)(128)(4,1)} %bitcast.247), calls=%async_computation.16 | async-start | bytes 8388608
  94.5 9.0 %copy-start.17 = (bf16[2,1,128,768]{3,2,1,0:T(8,128)(2,1)S(1)}, bf16[2,1,128,768]{3,2,1,0:T(8,128)(2,1)}, u32[]{:S(2)}) copy-start(bf16[2,1,128,768]{3,2,1,0:T(8,128)(2,1)} %get-tuple-element.104) | copy-start | bytes 1179652
  94.5 9.0 %slice-start.7 = ((s8[4718592]{0:T(1024)(128)(4,1)}), s8[524288]{0:T(1024)(128)(4,1)S(1)}, s32[]{:S(2)}) async-start(s8[4718592]{0:T(1024)(128)(4,1)} %bitcast.247), calls=%async_computation.17 | async-start | bytes 1048576
  108.1 14.5 %all-to-all-start.3 = ((bf16[2,2,128,768]{3,2,1,0:T(8,128)(2,1)}), bf16[2,2,128,768]{3,2,1,0:T(8,128)(2,1)}, u32[]{:S(2)}, u32[]{:S(2)}) async-start(bf16[2,2,128,768]{3,2,1,0:T(8,128)(2,1)} %copy.66), calls=%async_computation.4 | async-start | bytes 1572864 | tf_op jit(solution)/shard_map/all_to_all | solution.py:41
  112.4 111.2 %all-reduce.9.cloned.1.call-start = ((), (), s32[]{:S(2)}) async-start(), calls=%async_computation.9 | async-start | bytes 2359296 | tf_op jit(solution)/shard_map/psum | solution.py:262
  122.6 12.1 %copy-start.25 = (bf16[3,512,64]{1,2,0:T(8,128)(2,1)S(1)}, bf16[3,512,64]{1,2,0:T(8,128)(2,1)}, u32[]{:S(2)}) copy-start(bf16[3,512,64]{1,2,0:T(8,128)(2,1)} %copy-done.24) | copy-start | bytes 589828
  141.2 107.5 %reduce-scatter.5.cloned.1.call-start = ((), (), s32[]{:S(2)}) async-start(), calls=%async_computation.7 | async-start | bytes 983040 | tf_op jit(solution)/shard_map/reduce_scatter | solution.py:251
  143.9 294.6 %all-reduce.7.cloned.1.call-start = ((), (), s32[]{:S(2)}) async-start(), calls=%async_computation.8 | async-start | bytes 18874368 | tf_op jit(solution)/shard_map/psum | solution.py:190
  162.0 18.6 %copy-start.3 = (f32[128,768]{1,0:T(8,128)S(1)}, f32[128,768]{1,0:T(8,128)}, u32[]{:S(2)}) copy-start(f32[128,768]{1,0:T(8,128)} %copy-done.1) | copy-start | bytes 1179652
  163.0 17.2 %all-to-all-start.1 = ((bf16[2,2,128,768]{3,2,1,0:T(8,128)(2,1)}), bf16[2,2,128,768]{3,2,1,0:T(8,128)(2,1)S(1)}, u32[]{:S(2)}, u32[]{:S(2)}) async-start(bf16[2,2,128,768]{3,2,1,0:T(8,128)(2,1)} %copy.65), calls=%async_computation.2 | async-start | bytes 1572864 | tf_op jit(solution)/shard_map/all_to_all | solution.py:41
  180.2 68.4 %copy-start.4 = (bf16[1,128,768]{2,1,0:T(8,128)(2,1)S(1)}, bf16[1,128,768]{2,1,0:T(8,128)(2,1)}, u32[]{:S(2)}) copy-start(bf16[1,128,768]{2,1,0:T(8,128)(2,1)} %param.18) | copy-start | bytes 589828
  180.2 68.4 %copy-start.31 = (f32[768]{0:T(1024)S(1)}, f32[768]{0:T(1024)}, u32[]{:S(2)}) copy-start(f32[768]{0:T(1024)} %param.23) | copy-start | bytes 9220
  180.6 112.6 %copy-start.8 = (f32[128,768]{1,0:T(8,128)S(1)}, f32[128,768]{1,0:T(8,128)}, u32[]{:S(2)}) copy-start(f32[128,768]{1,0:T(8,128)} %copy-done.7) | copy-start | bytes 1179652
  180.6 112.6 %copy-start.10 = (bf16[1,128,768]{2,1,0:T(8,128)(2,1)S(1)}, bf16[1,128,768]{2,1,0:T(8,128)(2,1)}, u32[]{:S(2)}) copy-start(bf16[1,128,768]{2,1,0:T(8,128)(2,1)} %param.35) | copy-start | bytes 589828
  438.5 7.5 %copy-start.5 = (bf16[1,3072,768]{2,1,0:T(8,128)(2,1)S(1)}, bf16[1,3072,768]{2,1,0:T(8,128)(2,1)}, u32[]{:S(2)}) copy-start(bf16[1,3072,768]{2,1,0:T(8,128)(2,1)} %get-tuple-element.87) | copy-start | bytes 14155780
  (22 other events, 47.9 us)
Sparse Core Ops, SparseCore 0:
  31.1 28.8 reduce-scatter.2
  141.3 82.3 all-reduce.8
  226.2 22.3 reduce-scatter.4
  252.8 185.7 all-reduce.6
where the time goes:
time: 458 us; the launch traced here: 457 us
  waiting for transfers between devices  253 us (55%)
  matrix products  63.5 us (14%)
  blocking collectives  59.5 us (13%)
  other arithmetic  34.8 us (8%)
  starting transfers between devices  17.1 us (4%)
  local copies, waits for them, and re-layouts  14.9 us (3%)
  between operations  14.5 us (3%)
    psum x1, waiting for transfers between devices, local(): lax.psum(grad_in.astype(jnp.bfloat16), ('tp', 'dp')).astype(jnp.float32)  143 us
    dot_general x23, matrix products, contract(): lax.dot_general(left, right, (((left_dim,), (right_dim,)), ((), ())), pre...  59.8 us
    psum x1, waiting for transfers between devices, local(): lax.psum(joined_grad[:, :head_cols].astype(jnp.bfloat16), ('ep', 'dp'))  42.1 us
    psum x1, blocking collectives, local(): lax.psum((local_counts, ln1_gain_grad, ln1_bias_grad, ln2_gain_grad, ln2_...  41.6 us
    all_to_all x2, waiting for transfers between devices, to_sources(): return lax.all_to_all(buffer, 'ep', split_axis=0, concat_axis=0, tiled=True)  23.7 us
    reduce_scatter x1, waiting for transfers between devices, local(): lax.psum_scatter(contract(projected_grad, joined, 1, 1).astype(jnp.bfloat...  17.7 us
    reduce_scatter x1, waiting for transfers between devices, local(): lax.psum_scatter(contract(attn_heads, out_weight, 1, 0), 'tp', scatter_di...  16.9 us
    all_gather x1, blocking collectives, local(): piece = lax.all_gather(first_normed, 'tp', axis=0, tiled=True)  10.1 us
  transfers between devices with their start and end apart: 8, of which 7 were waited for; matrix products, arithmetic and copies ran while one was open for 10% of the time, Pallas kernels for 0%

commit v1 on v0

--- a/solution.py
+++ b/solution.py
@@ -259,7 +259,9 @@
     ](first_grad)
     tokens_grad = middle_grad + residual_part
     summed = (
-        lax.psum(joined_grad[:, :head_cols].astype(jnp.bfloat16), ("ep", "dp")).astype(jnp.float32),
+        jnp.sum(
+            lax.all_gather(joined_grad[:, :head_cols].astype(jnp.bfloat16), ("ep", "dp")), axis=0
+        ).astype(jnp.float32),
         lax.psum(
             joined_grad[:, head_cols : 2 * head_cols].astype(jnp.bfloat16), ("ep", "dp")
         ).astype(jnp.float32),

time: 458 us -> 505 us (1.10)
  waiting for transfers between devices: 253 us -> 296 us
    psum x1, waiting for transfers between devices: 143 us -> 182 us  [local(): lax.psum(grad_in.astype(jnp.bfloat16), ('tp', 'dp')).astype(jnp.float32)]
    all_gather x0 -> x1, waiting for transfers between devices: none -> 8.33 us  [local(): lax.all_gather(joined_grad[:, :head_cols].astype(jnp.bfloat16), ('ep', 'd...]
  transfers between devices with their start and end apart: 8 -> 9, of which waited for: 7 -> 8; matrix products, arithmetic and copies ran while one was open for 10% -> 10% of each run, Pallas kernels for 0% -> 0%
where the time goes in v1:
time: 505 us; the launch traced here: 504 us
  waiting for transfers between devices  296 us (59%)
  matrix products  63.6 us (13%)
  blocking collectives  59.8 us (12%)
  other arithmetic  35.5 us (7%)
  local copies, waits for them, and re-layouts  17.2 us (3%)
  starting transfers between devices  17.1 us (3%)
  between operations  14.6 us (3%)
    psum x1, waiting for transfers between devices, local(): lax.psum(grad_in.astype(jnp.bfloat16), ('tp', 'dp')).astype(jnp.float32)  182 us
    dot_general x23, matrix products, contract(): lax.dot_general(left, right, (((left_dim,), (right_dim,)), ((), ())), pre...  59.9 us
    psum x1, blocking collectives, local(): lax.psum((local_counts, ln1_gain_grad, ln1_bias_grad, ln2_gain_grad, ln2_...  41.9 us
    psum x1, waiting for transfers between devices, local(): lax.psum(joined_grad[:, head_cols:2 * head_cols].astype(jnp.bfloat16), ('...  37.9 us
    all_to_all x2, waiting for transfers between devices, to_sources(): return lax.all_to_all(buffer, 'ep', split_axis=0, concat_axis=0, tiled=True)  21.6 us
    reduce_scatter x1, waiting for transfers between devices, local(): lax.psum_scatter(contract(projected_grad, joined, 1, 1).astype(jnp.bfloat...  19.2 us
    reduce_scatter x1, waiting for transfers between devices, local(): lax.psum_scatter(contract(attn_heads, out_weight, 1, 0), 'tp', scatter_di...  16.9 us
  transfers between devices with their start and end apart: 9, of which 8 were waited for; matrix products, arithmetic and copies ran while one was open for 10% of the time, Pallas kernels for 0%

profile of v1, /device:TPU:0, one launch (start us, length us, event | category | flops | bytes accessed | tf_op | source)
XLA Modules:
  0.0 503.5 jit_solution(13059932257525367750)
XLA Ops:
  12.2 10.1 %all_gather.12 = bf16[512,768]{1,0:T(8,128)(2,1)S(1)} all-gather(bf16[128,768]{1,0:T(8,128)(2,1)S(1)} %fusion.83), channel_id=1, replica_groups=mesh['tp'=4,'ep'=2,'dp'=4] {'tp'}, dimensions={0}, use_global_device_ids=true | all-gather | bytes 983040 | tf_op jit(solution)/shard_map/all_gather | solution.py:89
  36.4 2.4 add_convert_fusion.2
  38.7 4.3 all-to-all-start.2
  43.0 16.9 %reduce-scatter.3.cloned.1.call-done = f32[128,768]{1,0:T(8,128)} async-done(((f32[512,768]{1,0:T(8,128)}), f32[128,768]{1,0:T(8,128)}) %reduce-scatter.3.cloned.1.call-update) | async-done | bytes 393232 | tf_op jit(solution)/shard_map/reduce_scatter | solution.py:128
  63.2 4.5 all-to-all-start
  67.7 2.0 fusion.128
  69.8 8.8 %all-to-all-done = bf16[2,2,128,768]{3,2,1,0:T(8,128)(2,1)} async-done(((bf16[2,2,128,768]{3,2,1,0:T(8,128)(2,1)}), bf16[2,2,128,768]{3,2,1,0:T(8,128)(2,1)}, u32[]{:S(2)}, u32[]{:S(2)}) %all-to-all-start) | async-done | bytes 786464 | tf_op jit(solution)/shard_map/all_to_all | solution.py:37
  79.9 11.0 %multiply_convert_fusion.2 = (bf16[256,3072]{1,0:T(8,128)(2,1)}, f32[256,3072]{1,0:T(8,128)S(1)}, f32[256,3072]{1,0:T(8,128)S(1)}) fusion(bf16[256,768]{1,0:T(8,128)(2,1)S(1)} %bitcast.237, bf16[1,768,3072]{2,1,0:T(8,128)(2,1)} %param.31), kind=kOutput, calls=%fused_computation.42 | convolution fusion | flops 1259077632 | bytes 12976128 | tf_op jit(solution)/shard_map/dot_general | solution.py:24
  91.0 2.1 add_convert_fusion.1
  94.6 9.0 %multiply_convert_fusion.1 = (bf16[256,3072]{1,0:T(8,128)(2,1)}, f32[256,3072]{1,0:T(8,128)S(1)}, f32[256,3072]{1,0:T(8,128)S(1)}) fusion(bf16[256,768]{1,0:T(8,128)(2,1)S(1)} %bitcast.221, bf16[1,768,3072]{2,1,0:T(8,128)(2,1)S(1)} %bitcast.250), kind=kOutput, calls=%fused_computation.29 | convolution fusion | flops 1259077632 | bytes 12976128 | tf_op jit(solution)/shard_map/dot_general | solution.py:24
  103.6 2.0 add_convert_fusion
  108.1 4.3 all-to-all-start.3
  112.5 10.0 %all-to-all-done.3 = bf16[2,2,128,768]{3,2,1,0:T(8,128)(2,1)} async-done(((bf16[2,2,128,768]{3,2,1,0:T(8,128)(2,1)}), bf16[2,2,128,768]{3,2,1,0:T(8,128)(2,1)}, u32[]{:S(2)}, u32[]{:S(2)}) %all-to-all-start.3) | async-done | bytes 786464 | tf_op jit(solution)/shard_map/all_to_all | solution.py:41
  126.9 7.8 %all_gather.13 = bf16[512,768]{1,0:T(8,128)(2,1)S(1)} all-gather(bf16[128,768]{1,0:T(8,128)(2,1)S(1)} %fusion.94), channel_id=1, replica_groups=mesh['tp'=4,'ep'=2,'dp'=4] {'tp'}, dimensions={0}, use_global_device_ids=true | all-gather | bytes 983040 | tf_op jit(solution)/shard_map/all_gather | solution.py:201
  141.2 2.7 convolution_convert_fusion.3
  144.8 5.2 %fusion.16 = bf16[1,768,3072]{2,1,0:T(8,128)(2,1)} fusion(bf16[256,768]{1,0:T(8,128)(2,1)S(1)} %bitcast.222, bf16[256,3072]{1,0:T(8,128)(2,1)} %copy-done.19), kind=kOutput, calls=%fused_computation.20 | convolution fusion | flops 1210318848 | bytes 6684672 | tf_op jit(solution)/shard_map/dot_general | solution.py:24
  150.0 3.6 fusion.17
  155.1 3.8 fusion.61
  158.8 3.8 fusion.58
  163.6 3.6 all-to-all-start.1
  167.2 11.5 %all-to-all-done.1 = bf16[2,2,128,768]{3,2,1,0:T(8,128)(2,1)S(1)} async-done(((bf16[2,2,128,768]{3,2,1,0:T(8,128)(2,1)}), bf16[2,2,128,768]{3,2,1,0:T(8,128)(2,1)S(1)}, u32[]{:S(2)}, u32[]{:S(2)}) %all-to-all-start.1) | async-done | bytes 786464 | tf_op jit(solution)/shard_map/all_to_all | solution.py:41
  180.1 37.9 %all-reduce.9.cloned.1.call-done = (bf16[768,192]{0,1:T(8,128)(2,1)}, bf16[768,192]{0,1:T(8,128)(2,1)}, bf16[192,768]{1,0:T(8,128)(2,1)}) async-done(((bf16[768,192]{0,1:T(8,128)(2,1)}, bf16[768,192]{0,1:T(8,128)(2,1)}, bf16[192,768]{1,0:T(8,128)(2,1)}), (bf16[768,192]{0,1:T(8,128)(2,1)}, bf16[768,192]{0,1:T(8,128)(2,1)}, bf16[192,768]{1,0:T(8,128)(2,1)})) %all-reduce.9.cloned.1.call-update) | async-done | bytes 884752 | tf_op jit(solution)/shard_map/psum | solution.py:265
  218.0 1.8 convert_element_type.165
  221.6 1.8 convert_element_type.168
  223.5 19.2 %reduce-scatter.5.cloned.1.call-done = bf16[128,768]{1,0:T(8,128)(2,1)} async-done(((bf16[512,768]{1,0:T(8,128)(2,1)}), bf16[128,768]{1,0:T(8,128)(2,1)}) %reduce-scatter.5.cloned.1.call-update) | async-done | bytes 196624 | tf_op jit(solution)/shard_map/reduce_scatter | solution.py:251
  245.1 41.9 %all-reduce.1 = (f32[768]{0:T(1024)}, f32[768]{0:T(1024)}, f32[768]{0:T(1024)}, f32[768]{0:T(1024)}, f32[4]{0:T(128)S(1)}) all-reduce(f32[768]{0:T(1024)S(1)} %get-tuple-element.61, f32[768]{0:T(1024)S(1)} %get-tuple-element.64, f32[768]{0:T(1024)S(1)} %get-tuple-element.59, ...), channel_id=1, replica_groups=mesh['tp'=4,'ep'=2,'dp'=4] {'tp','ep','dp'}, use_global_device_ids=true, to_apply=%region_17.18 | all-reduce | flops 3076 | bytes 24608 | tf_op jit(solution)/shard_map/psum | solution.py:273
  287.5 1.9 add_bitcast_fusion
  289.4 8.3 %all-gather.3.cloned.1.call-done = bf16[6144,192]{0,1:T(8,128)(2,1)} async-done(((bf16[768,192]{0,1:T(8,128)(2,1)}), bf16[6144,192]{0,1:T(8,128)(2,1)}) %all-gather.3.cloned.1.call-update) | async-done | bytes 2359312 | tf_op jit(solution)/shard_map/all_gather | solution.py:263
  297.8 2.3 copy.75
  302.6 182.3 %all-reduce.7.cloned.1.call-done = (bf16[1,768,3072]{2,1,0:T(8,128)(2,1)}, bf16[1,3072,768]{2,1,0:T(8,128)(2,1)}) async-done(((bf16[1,768,3072]{2,1,0:T(8,128)(2,1)}, bf16[1,3072,768]{2,1,0:T(8,128)(2,1)}), (bf16[1,768,3072]{2,1,0:T(8,128)(2,1)}, bf16[1,3072,768]{2,1,0:T(8,128)(2,1)})) %all-reduce.7.cloned.1.call-update) | async-done | bytes 9437200 | tf_op jit(solution)/shard_map/psum | solution.py:190
  485.0 7.5 %broadcast_in_dim.113 = f32[1,768,3072]{2,1,0:T(8,128)} convert(bf16[1,768,3072]{2,1,0:T(8,128)(2,1)} %get-tuple-element.86) | non-fusion elementwise | flops 2359296 | bytes 14155776 | tf_op jit(solution)/shard_map/broadcast_in_dim | solution.py:288
  492.5 4.5 broadcast_in_dim.115
  (181 shorter events, 50.1 us)
Async XLA Ops:
  7.2 22.2 %copy-start = (bf16[192,768]{1,0:T(8,128)(2,1)S(1)}, bf16[192,768]{1,0:T(8,128)(2,1)}, u32[]{:S(2)}) copy-start(bf16[192,768]{1,0:T(8,128)(2,1)} %param.28) | copy-start | bytes 884740
  7.2 17.2 %copy-start.27 = (bf16[768,192]{0,1:T(8,128)(2,1)S(1)}, bf16[768,192]{0,1:T(8,128)(2,1)}, u32[]{:S(2)}) copy-start(bf16[768,192]{0,1:T(8,128)(2,1)} %param.27) | copy-start | bytes 884740
  7.2 52.7 %reduce-scatter.3.cloned.1.call-start = ((), (), s32[]{:S(2)}) async-start(), calls=%async_computation.6 | async-start | bytes 1966080 | tf_op jit(solution)/shard_map/reduce_scatter | solution.py:128
  12.2 14.0 %copy-start.33 = (s32[1,512]{1,0:T(1,128)S(1)}, s32[1,512]{1,0:T(1,128)}, u32[]{:S(2)}) copy-start(s32[1,512]{1,0:T(1,128)} %param.19) | copy-start | bytes 6148
  36.3 25.5 %copy-start.32 = (f32[768]{0:T(1024)S(1)}, f32[768]{0:T(1024)}, u32[]{:S(2)}) copy-start(f32[768]{0:T(1024)} %param.29) | copy-start | bytes 9220
  36.3 25.5 %copy-start.34 = (f32[768]{0:T(1024)S(1)}, f32[768]{0:T(1024)}, u32[]{:S(2)}) copy-start(f32[768]{0:T(1024)} %param.30) | copy-start | bytes 9220
  38.7 24.5 %all-to-all-start.2 = ((bf16[2,2,128,768]{3,2,1,0:T(8,128)(2,1)}), bf16[2,2,128,768]{3,2,1,0:T(8,128)(2,1)}, u32[]{:S(2)}, u32[]{:S(2)}) async-start(bf16[2,2,128,768]{3,2,1,0:T(8,128)(2,1)} %bitcast.219), calls=%async_computation.3 | async-start | bytes 1572864 | tf_op jit(solution)/shard_map/all_to_all | solution.py:37
  63.2 15.3 %all-to-all-start = ((bf16[2,2,128,768]{3,2,1,0:T(8,128)(2,1)}), bf16[2,2,128,768]{3,2,1,0:T(8,128)(2,1)}, u32[]{:S(2)}, u32[]{:S(2)}) async-start(bf16[2,2,128,768]{3,2,1,0:T(8,128)(2,1)} %bitcast.218), calls=%async_computation.1 | async-start | bytes 1572864 | tf_op jit(solution)/shard_map/all_to_all | solution.py:37
  78.6 12.4 %slice-start.4 = ((s8[4718592]{0:T(1024)(128)(4,1)}), s8[4194304]{0:T(1024)(128)(4,1)S(1)}, s32[]{:S(2)}) async-start(s8[4718592]{0:T(1024)(128)(4,1)} %bitcast.251), calls=%async_computation.15 | async-start | bytes 8388608
  78.6 14.5 %slice-start = ((s8[4718592]{0:T(1024)(128)(4,1)}), s8[4194304]{0:T(1024)(128)(4,1)S(1)}, s32[]{:S(2)}) async-start(s8[4718592]{0:T(1024)(128)(4,1)} %bitcast.247), calls=%async_computation.11 | async-start | bytes 8388608
  78.6 16.0 %slice-start.2 = ((s8[4718592]{0:T(1024)(128)(4,1)}), s8[4194304]{0:T(1024)(128)(4,1)S(1)}, s32[]{:S(2)}) async-start(s8[4718592]{0:T(1024)(128)(4,1)} %bitcast.249), calls=%async_computation.13 | async-start | bytes 8388608
  79.9 14.6 %copy-start.11 = (bf16[2,1,128,768]{3,2,1,0:T(8,128)(2,1)}, bf16[2,1,128,768]{3,2,1,0:T(8,128)(2,1)S(1)}, u32[]{:S(2)}) copy-start(bf16[2,1,128,768]{3,2,1,0:T(8,128)(2,1)S(1)} %get-tuple-element.105) | copy-start | bytes 1179652
  79.9 11.1 %copy-start.26 = (bf16[2,1,128,768]{3,2,1,0:T(8,128)(2,1)S(1)}, bf16[2,1,128,768]{3,2,1,0:T(8,128)(2,1)}, u32[]{:S(2)}) copy-start(bf16[2,1,128,768]{3,2,1,0:T(8,128)(2,1)} %get-tuple-element.102) | copy-start | bytes 1179652
  79.9 11.1 %slice-start.5 = ((s8[4718592]{0:T(1024)(128)(4,1)}), s8[524288]{0:T(1024)(128)(4,1)S(1)}, s32[]{:S(2)}) async-start(s8[4718592]{0:T(1024)(128)(4,1)} %bitcast.251), calls=%async_computation.16 | async-start | bytes 1048576
  79.9 13.1 %slice-start.1 = ((s8[4718592]{0:T(1024)(128)(4,1)}), s8[524288]{0:T(1024)(128)(4,1)S(1)}, s32[]{:S(2)}) async-start(s8[4718592]{0:T(1024)(128)(4,1)} %bitcast.247), calls=%async_computation.12 | async-start | bytes 1048576
  79.9 14.6 %slice-start.3 = ((s8[4718592]{0:T(1024)(128)(4,1)}), s8[524288]{0:T(1024)(128)(4,1)S(1)}, s32[]{:S(2)}) async-start(s8[4718592]{0:T(1024)(128)(4,1)} %bitcast.249), calls=%async_computation.14 | async-start | bytes 1048576
  93.1 10.5 %slice-start.6 = ((s8[4718592]{0:T(1024)(128)(4,1)}), s8[4194304]{0:T(1024)(128)(4,1)S(1)}, s32[]{:S(2)}) async-start(s8[4718592]{0:T(1024)(128)(4,1)} %bitcast.253), calls=%async_computation.17 | async-start | bytes 8388608
  94.5 9.0 %copy-start.17 = (bf16[2,1,128,768]{3,2,1,0:T(8,128)(2,1)S(1)}, bf16[2,1,128,768]{3,2,1,0:T(8,128)(2,1)}, u32[]{:S(2)}) copy-start(bf16[2,1,128,768]{3,2,1,0:T(8,128)(2,1)} %get-tuple-element.103) | copy-start | bytes 1179652
  94.6 9.0 %slice-start.7 = ((s8[4718592]{0:T(1024)(128)(4,1)}), s8[524288]{0:T(1024)(128)(4,1)S(1)}, s32[]{:S(2)}) async-start(s8[4718592]{0:T(1024)(128)(4,1)} %bitcast.253), calls=%async_computation.18 | async-start | bytes 1048576
  108.1 14.4 %all-to-all-start.3 = ((bf16[2,2,128,768]{3,2,1,0:T(8,128)(2,1)}), bf16[2,2,128,768]{3,2,1,0:T(8,128)(2,1)}, u32[]{:S(2)}, u32[]{:S(2)}) async-start(bf16[2,2,128,768]{3,2,1,0:T(8,128)(2,1)} %copy.66), calls=%async_computation.4 | async-start | bytes 1572864 | tf_op jit(solution)/shard_map/all_to_all | solution.py:41
  112.4 105.6 %all-reduce.9.cloned.1.call-start = ((), (), s32[]{:S(2)}) async-start(), calls=%async_computation.10 | async-start | bytes 1769472 | tf_op jit(solution)/shard_map/psum | solution.py:265
  122.6 12.1 %copy-start.25 = (bf16[3,512,64]{1,2,0:T(8,128)(2,1)S(1)}, bf16[3,512,64]{1,2,0:T(8,128)(2,1)}, u32[]{:S(2)}) copy-start(bf16[3,512,64]{1,2,0:T(8,128)(2,1)} %copy-done.24) | copy-start | bytes 589828
  141.2 101.5 %reduce-scatter.5.cloned.1.call-start = ((), (), s32[]{:S(2)}) async-start(), calls=%async_computation.7 | async-start | bytes 983040 | tf_op jit(solution)/shard_map/reduce_scatter | solution.py:251
  143.9 153.9 %all-gather.3.cloned.1.call-start = ((), (), s32[]{:S(2)}) async-start(), calls=%async_computation.8 | async-start | bytes 2654208 | tf_op jit(solution)/shard_map/all_gather | solution.py:263
  144.5 340.4 %all-reduce.7.cloned.1.call-start = ((), (), s32[]{:S(2)}) async-start(), calls=%async_computation.9 | async-start | bytes 18874368 | tf_op jit(solution)/shard_map/psum | solution.py:190
  162.6 16.5 %copy-start.3 = (f32[128,768]{1,0:T(8,128)S(1)}, f32[128,768]{1,0:T(8,128)}, u32[]{:S(2)}) copy-start(f32[128,768]{1,0:T(8,128)} %copy-done.1) | copy-start | bytes 1179652
  163.6 15.1 %all-to-all-start.1 = ((bf16[2,2,128,768]{3,2,1,0:T(8,128)(2,1)}), bf16[2,2,128,768]{3,2,1,0:T(8,128)(2,1)S(1)}, u32[]{:S(2)}, u32[]{:S(2)}) async-start(bf16[2,2,128,768]{3,2,1,0:T(8,128)(2,1)} %copy.65), calls=%async_computation.2 | async-start | bytes 1572864 | tf_op jit(solution)/shard_map/all_to_all | solution.py:41
  167.2 75.5 %copy-start.4 = (bf16[1,128,768]{2,1,0:T(8,128)(2,1)S(1)}, bf16[1,128,768]{2,1,0:T(8,128)(2,1)}, u32[]{:S(2)}) copy-start(bf16[1,128,768]{2,1,0:T(8,128)(2,1)} %param.18) | copy-start | bytes 589828
  167.2 75.5 %copy-start.31 = (f32[768]{0:T(1024)S(1)}, f32[768]{0:T(1024)}, u32[]{:S(2)}) copy-start(f32[768]{0:T(1024)} %param.23) | copy-start | bytes 9220
  178.7 108.8 %copy-start.8 = (f32[128,768]{1,0:T(8,128)S(1)}, f32[128,768]{1,0:T(8,128)}, u32[]{:S(2)}) copy-start(f32[128,768]{1,0:T(8,128)} %copy-done.7) | copy-start | bytes 1179652
  178.7 108.8 %copy-start.10 = (bf16[1,128,768]{2,1,0:T(8,128)(2,1)S(1)}, bf16[1,128,768]{2,1,0:T(8,128)(2,1)}, u32[]{:S(2)}) copy-start(bf16[1,128,768]{2,1,0:T(8,128)(2,1)} %param.35) | copy-start | bytes 589828
  485.0 7.5 %copy-start.5 = (bf16[1,3072,768]{2,1,0:T(8,128)(2,1)S(1)}, bf16[1,3072,768]{2,1,0:T(8,128)(2,1)}, u32[]{:S(2)}) copy-start(bf16[1,3072,768]{2,1,0:T(8,128)(2,1)} %get-tuple-element.87) | copy-start | bytes 14155780
  (23 other events, 54.8 us)
Sparse Core Ops, SparseCore 0:
  31.1 28.8 reduce-scatter.2
  141.3 76.6 all-reduce.8
  220.5 22.0 reduce-scatter.4
  244.8 52.9 all-gather.2
  301.9 183.0 all-reduce.6
